TPU v7x, 256 devices: a whole 4x4x8 slice. The times are simulated.
256 devices in a mesh: expert: 32 (over x, z), tensor: 8 (over y, core).
Axes of the slice: x: 4, y: 4, z: 8, core: 2. Of those that a mesh axis runs over, the one named last changes fastest.
Arguments:
- tokens: bfloat16 [8192, 4096], P('expert'), may hold values from -6 to 6
- cotangent: bfloat16 [8192, 4096], P('expert'), may hold values from -1.5 to 1.5
- w_in: bfloat16 [4096, 65536], P(None, ('expert', 'tensor')), may hold values from -0.09375 to 0.09375
- w_out: bfloat16 [65536, 4096], P(('expert', 'tensor')), may hold values from -0.09375 to 0.09375
- router: bfloat16 [4096, 16], replicated, may hold values from -0.09375 to 0.09375
- chosen: int32 [16, 512], replicated, may hold values from 0 to 8191, as said below
Outputs:
- grad_tokens: bfloat16 [8192, 4096], P('expert', 'tensor')
- grad_in: bfloat16 [4096, 65536], P(None, ('expert', 'tensor'))
- grad_out: bfloat16 [65536, 4096], P(('expert', 'tensor'))
- grad_router: float32 [4096, 16], replicated
Inputs may be any that keep to these rules, and one draw needn't show every extreme that they name: Row e lists, in increasing order, 512 distinct tokens chosen by expert e; at most 32 of them lie among one device's 256 consecutive tokens, and in every row some device's tokens hold exactly 32 of them.
All inputs are finite; a program needn't handle non-finite values.
Results may differ from a plain program's by a relative error of at most 0.005.
Values may be sent and summed in bfloat16 or wider, within the bound.
A program may use at most 128 MiB of HBM per device.

v0:
```python
import jax
import jax.numpy as jnp
from jax import lax
from jax.sharding import PartitionSpec as P


def body(tokens, cotangent, w_in, w_out, router, chosen):
    tok_dev, features = tokens.shape
    n_expert = lax.axis_size("expert")
    bucket = 4 * tok_dev // n_expert
    capacity = chosen.shape[1]
    expert_total = router.shape[1]
    device_index = lax.axis_index("expert")
    expert = device_index // 2
    slot_range = jnp.arange(bucket, dtype=jnp.int32)
    first_token = device_index * tok_dev
    starts = jnp.sum((chosen < first_token).astype(jnp.int32), axis=1)
    run_ends = jnp.sum((chosen < first_token + tok_dev).astype(jnp.int32), axis=1)
    counts = run_ends - starts
    positions = jnp.minimum(starts[:, None] + slot_range[None, :], capacity - 1)
    picked = jnp.take_along_axis(chosen, positions, axis=1) - first_token
    filled = slot_range[None, :] < counts[:, None]
    local_rows = jnp.where(filled, picked, 0)
    owner_expert = jnp.arange(n_expert, dtype=jnp.int32) // 2
    send_rows = local_rows[owner_expert].reshape(-1)
    send_filled = filled[owner_expert].reshape(-1)

    def pack(source):
        gathered = jnp.where(send_filled[:, None], source[send_rows], jnp.zeros((), source.dtype))
        return gathered.reshape(n_expert, bucket, source.shape[1])

    got_x, got_y = (
        lax.all_to_all(pack(tokens), "expert", split_axis=0, concat_axis=0, tiled=True),
        lax.all_to_all(pack(cotangent), "expert", split_axis=0, concat_axis=0, tiled=True),
    )
    my_chosen = lax.dynamic_index_in_dim(chosen, expert, 0, keepdims=False)
    home_index = my_chosen // tok_dev
    bounds = jnp.arange(n_expert, dtype=jnp.int32) * tok_dev
    run_start = jnp.sum((my_chosen[None, :] < bounds[:, None]).astype(jnp.int32), axis=1)
    slot_index = home_index * bucket + jnp.arange(capacity, dtype=jnp.int32) - run_start[home_index]
    x_rows = got_x.reshape(-1, features)[slot_index]
    grad_rows = got_y.reshape(-1, features)[slot_index]
    r_col = lax.dynamic_slice_in_dim(router, expert, 1, 1)
    gate = jax.nn.sigmoid(jnp.dot(x_rows, r_col, preferred_element_type=jnp.float32)[:, 0])
    pre_act = jnp.dot(x_rows, w_in, preferred_element_type=jnp.float32)
    sig_act = jax.nn.sigmoid(pre_act)
    hidden = pre_act * sig_act
    upstream = jnp.dot(grad_rows, w_out.T, preferred_element_type=jnp.float32)
    gated_hidden = (gate[:, None] * hidden).astype(jnp.bfloat16)
    gate_grad = jnp.sum(hidden * upstream, axis=1)
    pre_grad = (gate[:, None] * upstream * sig_act * (1.0 + pre_act * (1.0 - sig_act))).astype(
        jnp.bfloat16
    )
    grad_out = jnp.dot(gated_hidden.T, grad_rows, preferred_element_type=jnp.float32).astype(
        jnp.bfloat16
    )
    grad_in = jnp.dot(x_rows.T, pre_grad, preferred_element_type=jnp.float32).astype(jnp.bfloat16)
    score_grad = gate_grad * gate * (1.0 - gate)
    router_col = jnp.dot(score_grad, x_rows.astype(jnp.float32), precision=lax.Precision.HIGHEST)
    router_term = (
        router_col[:, None] * (jnp.arange(expert_total) == expert).astype(jnp.float32)[None, :]
    )
    grad_router = lax.psum(router_term, ("expert", "tensor"))
    router_rows = r_col.astype(jnp.float32)
    summed = lax.psum_scatter(
        jnp.dot(w_in, pre_grad.T, preferred_element_type=jnp.float32)
        + router_rows * score_grad[None, :],
        "tensor",
        scatter_dimension=0,
        tiled=True,
    )
    share = summed.shape[0]
    outgoing = jnp.zeros((share, n_expert * bucket), jnp.float32).at[:, slot_index].set(summed)
    returned = lax.all_to_all(
        outgoing.reshape(share, n_expert, bucket), "expert", split_axis=1, concat_axis=1, tiled=True
    )
    returned = jnp.where(send_filled[None, :], returned.reshape(share, -1), 0.0)
    combined = jnp.zeros((share, tok_dev), jnp.float32).at[:, send_rows].add(returned)
    grad_tokens = combined.T.astype(jnp.bfloat16)
    return (grad_tokens, grad_in, grad_out, grad_router)


def solution(mesh):
    placed = (
        P("expert", None),
        P("expert", None),
        P(None, ("expert", "tensor")),
        P(("expert", "tensor"), None),
        P(),
        P(),
    )
    return jax.shard_map(
        body,
        mesh=mesh,
        in_specs=placed,
        out_specs=(
            P("expert", "tensor"),
            P(None, ("expert", "tensor")),
            P(("expert", "tensor"), None),
            P(),
        ),
        check_vma=False,
    )
```

profile of v0, /device:TPU:2, one launch (start us, length us, event | category | flops | bytes accessed | tf_op | source)
XLA Modules:
  0.0 806.7 jit_solution(2339139497223671526)
XLA Ops:
  8.1 1.0 convert_reduce_fusion.2
  9.2 4.5 gather_fusion.6
  15.3 7.8 gather_fusion.4
  23.1 16.9 %gather_fusion.2 = bf16[1024,4096]{1,0:T(8,128)(2,1)} fusion(bf16[256,4096]{1,0:T(8,128)(2,1)} %param.6, s32[1024]{0:T(1024)S(1)} %broadcast_clamp_fusion), kind=kCustom, calls=%fused_computation.2 | custom fusion | bytes 16781312 | tf_op jit(solution)/shard_map/gather | solution.py:29
  40.0 9.2 %broadcast_select_fusion = (bf16[32,32,4096]{2,1,0:T(8,128)(2,1)}, bf16[32,32,4096]{2,1,0:T(8,128)(2,1)S(1)}) fusion(bf16[32,32,4096]{2,1,0:T(8,128)(2,1)} %bitcast.83, pred[32,32]{1,0:T(8,128)(4,1)S(1)} %gather_fusion.1, bf16[32,32,4096]{2,1,0:T(8,128)(2,1)} %bitcast.84), kind=kLoop, calls=%fused_computation.10 | loop fusion | flops 8388608 | bytes 33555456 | tf_op jit(solution)/shard_map/jit(_where)/select_n | solution.py:29
  49.2 194.9 %all_to_all.15 = bf16[32,32,4096]{2,1,0:T(8,128)(2,1)} all-to-all(bf16[32,32,4096]{2,1,0:T(8,128)(2,1)S(1)} %get-tuple-element.37), channel_id=1, replica_groups=mesh['expert'=32,'tensor'=8] {'expert'}, dimensions={0} | all-to-all | bytes 16777216 | tf_op jit(solution)/shard_map/all_to_all | solution.py:33
  244.1 7.7 all-to-all-start.1
  251.9 0.9 dynamic-slice_reduce_fusion
  253.0 0.7 fusion.21
  253.7 4.3 compare_select_fusion.5
  258.1 0.7 fusion.20
  258.9 15.5 %select_select_fusion = s32[512]{0:T(512)S(1)} fusion(pred[512]{0:T(512)(128)(4,1)S(1)} %get-tuple-element.30, pred[512]{0:T(512)(128)(4,1)S(1)} %get-tuple-element.29, pred[512]{0:T(512)(128)(4,1)S(1)} %get-tuple-element.28, pred[512]{0:T(512)(128)(4,1)S(1)} %get-tuple-element.27, pred[512]{0:T(512)(128)(4,1)S(1)} %get-tuple-element.26, ...), kind=kLoop, calls=%fused_computation.88 | loop fusion | flops 12800 | bytes 16996 | tf_op jit(solution)/shard_map/gather | solution.py:40
  274.5 13.3 %gather_fusion.3 = bf16[512,4096]{1,0:T(8,128)(2,1)} fusion(bf16[1024,4096]{1,0:T(8,128)(2,1)} %bitcast.82, s32[1024]{0:T(1024)S(1)} %pad_clamp_fusion), kind=kCustom, calls=%fused_computation.3 | custom fusion | bytes 8390656 | tf_op jit(solution)/shard_map/gather | solution.py:41
  287.9 3.5 fusion.9
  291.4 1.3 fusion.22
  292.7 144.1 %all-to-all-done.1 = bf16[32,32,4096]{2,1,0:T(8,128)(2,1)} async-done(((bf16[32,32,4096]{2,1,0:T(8,128)(2,1)}), bf16[32,32,4096]{2,1,0:T(8,128)(2,1)}, u32[]{:S(2)}, u32[]{:S(2)}) %all-to-all-start.1) | async-done | bytes 8388640 | tf_op jit(solution)/shard_map/all_to_all | solution.py:34
  436.9 13.0 %gather_fusion.5 = bf16[512,4096]{1,0:T(8,128)(2,1)} fusion(bf16[1024,4096]{1,0:T(8,128)(2,1)} %bitcast.43, s32[1024]{0:T(1024)S(1)} %pad_clamp_fusion), kind=kCustom, calls=%fused_computation.5 | custom fusion | bytes 8390656 | tf_op jit(solution)/shard_map/gather | solution.py:42
  449.9 4.3 multiply_reduce_fusion
  454.2 5.1 bitcast_add_fusion
  459.3 57.6 %reduce-scatter.2.cloned.1.call-done = f32[512,512]{0,1:T(8,128)} async-done(((f32[4096,512]{0,1:T(8,128)}), f32[512,512]{0,1:T(8,128)}) %reduce-scatter.2.cloned.1.call-update) | async-done | bytes 1048592 | tf_op jit(solution)/shard_map/reduce_scatter | solution.py:65
  517.0 4.4 scatter_custom_fusion
  521.4 10.2 %all-to-all-start.2 = ((f32[512,32,32]{0,2,1:T(8,128)}), f32[512,32,32]{0,2,1:T(8,128)}, u32[]{:S(2)}, u32[]{:S(2)}) async-start(f32[512,32,32]{0,2,1:T(8,128)} %bitcast.46), calls=%async_computation.3 | async-start | bytes 4194304 | tf_op jit(solution)/shard_map/all_to_all | solution.py:74
  531.7 3.9 fusion.23
  535.6 0.8 broadcast_multiply_fusion
  536.5 5.0 convolution_convert_fusion.1
  541.4 2.6 convolution_convert_fusion
  544.1 34.9 %all-to-all-done.2 = f32[512,32,32]{0,2,1:T(8,128)} async-done(((f32[512,32,32]{0,2,1:T(8,128)}), f32[512,32,32]{0,2,1:T(8,128)}, u32[]{:S(2)}, u32[]{:S(2)}) %all-to-all-start.2) | async-done | bytes 2097184 | tf_op jit(solution)/shard_map/all_to_all | solution.py:74
  579.0 3.2 bitcast_select_fusion
  582.2 7.6 scatter_custom_fusion.1
  589.8 0.7 convert_bitcast_fusion
  590.5 207.0 %all-reduce.2.cloned.1.call-done = f32[4096,16]{0,1:T(8,128)} async-done(((f32[4096,16]{0,1:T(8,128)}), f32[4096,16]{0,1:T(8,128)}) %all-reduce.2.cloned.1.call-update) | async-done | bytes 262160 | tf_op jit(solution)/shard_map/psum | solution.py:63
  797.6 1.7 copy.11
  (40 shorter events, 2.3 us)
Async XLA Ops:
  8.0 7.3 copy-start
  8.0 1.2 copy-start.2
  244.1 192.7 %all-to-all-start.1 = ((bf16[32,32,4096]{2,1,0:T(8,128)(2,1)}), bf16[32,32,4096]{2,1,0:T(8,128)(2,1)}, u32[]{:S(2)}, u32[]{:S(2)}) async-start(bf16[32,32,4096]{2,1,0:T(8,128)(2,1)} %get-tuple-element.36), calls=%async_computation.1 | async-start | bytes 16777216 | tf_op jit(solution)/shard_map/all_to_all | solution.py:34
  251.8 265.1 %reduce-scatter.2.cloned.1.call-start = ((), (), s32[]{:S(2)}) async-start(), calls=%async_computation.4 | async-start | bytes 9437184 | tf_op jit(solution)/shard_map/reduce_scatter | solution.py:65
  274.5 16.9 %copy-start.5 = (bf16[4096,256]{1,0:T(8,128)(2,1)S(1)}, bf16[4096,256]{1,0:T(8,128)(2,1)}, u32[]{:S(2)}) copy-start(bf16[4096,256]{1,0:T(8,128)(2,1)} %param.8) | copy-start | bytes 6291460
  287.9 3.5 copy-start.3
  521.4 57.6 %all-to-all-start.2 = ((f32[512,32,32]{0,2,1:T(8,128)}), f32[512,32,32]{0,2,1:T(8,128)}, u32[]{:S(2)}, u32[]{:S(2)}) async-start(f32[512,32,32]{0,2,1:T(8,128)} %bitcast.46), calls=%async_computation.3 | async-start | bytes 4194304 | tf_op jit(solution)/shard_map/all_to_all | solution.py:74
  531.6 266.0 %all-reduce.2.cloned.1.call-start = ((), (), s32[]{:S(2)}) async-start(), calls=%async_computation.5 | async-start | bytes 524288 | tf_op jit(solution)/shard_map/psum | solution.py:63
  536.5 5.0 copy-start.4
  541.4 257.8 %copy-start.1 = (bf16[256,4096]{1,0:T(8,128)(2,1)S(1)}, bf16[256,4096]{1,0:T(8,128)(2,1)}, u32[]{:S(2)}) copy-start(bf16[256,4096]{1,0:T(8,128)(2,1)} %param.7) | copy-start | bytes 6291460
Sparse Core Ops, SparseCore 0:
  459.4 57.4 reduce-scatter.1
Sparse Core Ops, SparseCore 1:
  538.1 259.4 all-reduce.1
where the time goes:
time: 808 us; the launch traced here: 807 us
  waiting for transfers between devices  444 us (55%)
  blocking collectives  195 us (24%)
  local copies, waits for them, and re-layouts  65.6 us (8%)
  other arithmetic  43 us (5%)
  matrix products  25.8 us (3%)
  starting transfers between devices  18 us (2%)
  between operations  15.7 us (2%)
    psum x1, waiting for transfers between devices, body(): grad_router = lax.psum(router_term, ('expert', 'tensor'))  207 us
    all_to_all x1, blocking collectives, body(): lax.all_to_all(pack(tokens), 'expert', split_axis=0, concat_axis=0, tiled...  195 us
    all_to_all x1, waiting for transfers between devices, body(): lax.all_to_all(pack(cotangent), 'expert', split_axis=0, concat_axis=0, ti...  144 us
    reduce_scatter x1, waiting for transfers between devices, body(): lax.psum_scatter(jnp.dot(w_in, pre_grad.T, preferred_element_type=jnp.flo...  57.6 us
    all_to_all x1, waiting for transfers between devices, body(): lax.all_to_all(outgoing.reshape(share, n_expert, bucket), 'expert', split...  34.9 us
    gather x2, local copies, waits for them, and re-layouts, pack(): source[send_rows]  24.8 us
    gather x3, other arithmetic, body(): run_start[home_index]  20 us
  transfers between devices with their start and end apart: 4, of which 4 were waited for; matrix products, arithmetic and copies ran while one was open for 8% of the time, Pallas kernels for 0%

commit v1 on v0

--- a/solution.py
+++ b/solution.py
@@ -60,7 +60,7 @@
     router_term = (
         router_col[:, None] * (jnp.arange(expert_total) == expert).astype(jnp.float32)[None, :]
     )
-    grad_router = lax.psum(router_term, ("expert", "tensor"))
+    grad_router = jnp.sum(lax.all_gather(router_term, ("expert", "tensor")), axis=0)
     router_rows = r_col.astype(jnp.float32)
     summed = lax.psum_scatter(
         jnp.dot(w_in, pre_grad.T, preferred_element_type=jnp.float32)

time: 808 us -> 755 us (0.934)
  waiting for transfers between devices: 444 us -> 372 us
  other arithmetic: 43 us -> 63.3 us
    psum x1 -> x0, waiting for transfers between devices: 207 us -> none  [body(): grad_router = lax.psum(router_term, ('expert', 'tensor'))]
    all_gather x0 -> x1, waiting for transfers between devices: none -> 116 us  [body(): lax.all_gather(router_term, ('expert', 'tensor'))]
    reduce_sum x0 -> x1, other arithmetic: none -> 21.8 us  [body(): jnp.sum(lax.all_gather(router_term, ('expert', 'tensor')), axis=0)]
    all_to_all x1, waiting for transfers between devices: 34.9 us -> 56.2 us  [body(): lax.all_to_all(outgoing.reshape(share, n_expert, bucket), 'expert', split...]
  transfers between devices with their start and end apart: 4 -> 4, of which waited for: 4 -> 4; matrix products, arithmetic and copies ran while one was open for 8% -> 9% of each run, Pallas kernels for 0% -> 0%
where the time goes in v1:
time: 755 us; the launch traced here: 753 us
  waiting for transfers between devices  372 us (49%)
  blocking collectives  195 us (26%)
  local copies, waits for them, and re-layouts  64.2 us (9%)
  other arithmetic  63.3 us (8%)
  matrix products  25.7 us (3%)
  starting transfers between devices  17.9 us (2%)
  between operations  15.7 us (2%)
    all_to_all x1, blocking collectives, body(): lax.all_to_all(pack(tokens), 'expert', split_axis=0, concat_axis=0, tiled...  195 us
    all_to_all x1, waiting for transfers between devices, body(): lax.all_to_all(pack(cotangent), 'expert', split_axis=0, concat_axis=0, ti...  144 us
    all_gather x1, waiting for transfers between devices, body(): lax.all_gather(router_term, ('expert', 'tensor'))  116 us
    all_to_all x1, waiting for transfers between devices, body(): lax.all_to_all(outgoing.reshape(share, n_expert, bucket), 'expert', split...  56.2 us
    reduce_scatter x1, waiting for transfers between devices, body(): lax.psum_scatter(jnp.dot(w_in, pre_grad.T, preferred_element_type=jnp.flo...  55.6 us
    gather x2, local copies, waits for them, and re-layouts, pack(): source[send_rows]  24.8 us
    reduce_sum x1, other arithmetic, body(): jnp.sum(lax.all_gather(router_term, ('expert', 'tensor')), axis=0)  21.8 us
    gather x3, other arithmetic, body(): run_start[home_index]  20 us
  transfers between devices with their start and end apart: 4, of which 4 were waited for; matrix products, arithmetic and copies ran while one was open for 9% of the time, Pallas kernels for 0%

profile of v1, /device:TPU:2, one launch (start us, length us, event | category | flops | bytes accessed | tf_op | source)
XLA Modules:
  0.0 753.4 jit_solution(3489701042617409861)
XLA Ops:
  8.1 1.0 convert_reduce_fusion.2
  9.2 4.5 gather_fusion.6
  15.3 7.8 %gather_fusion.4 = bf16[1024,4096]{1,0:T(8,128)(2,1)} fusion(bf16[256,4096]{1,0:T(8,128)(2,1)S(1)} %copy-done, s32[1024]{0:T(1024)S(1)} %broadcast_clamp_fusion), kind=kCustom, calls=%fused_computation.4 | custom fusion | bytes 16781312 | tf_op jit(solution)/shard_map/gather | solution.py:29
  23.1 16.9 %gather_fusion.2 = bf16[1024,4096]{1,0:T(8,128)(2,1)} fusion(bf16[256,4096]{1,0:T(8,128)(2,1)} %param.6, s32[1024]{0:T(1024)S(1)} %broadcast_clamp_fusion), kind=kCustom, calls=%fused_computation.2 | custom fusion | bytes 16781312 | tf_op jit(solution)/shard_map/gather | solution.py:29
  40.0 9.2 %broadcast_select_fusion = (bf16[32,32,4096]{2,1,0:T(8,128)(2,1)}, bf16[32,32,4096]{2,1,0:T(8,128)(2,1)S(1)}) fusion(bf16[32,32,4096]{2,1,0:T(8,128)(2,1)} %bitcast.83, pred[32,32]{1,0:T(8,128)(4,1)S(1)} %gather_fusion.1, bf16[32,32,4096]{2,1,0:T(8,128)(2,1)} %bitcast.84), kind=kLoop, calls=%fused_computation.10 | loop fusion | flops 8388608 | bytes 33555456 | tf_op jit(solution)/shard_map/jit(_where)/select_n | solution.py:29
  49.2 194.9 %all_to_all.15 = bf16[32,32,4096]{2,1,0:T(8,128)(2,1)} all-to-all(bf16[32,32,4096]{2,1,0:T(8,128)(2,1)S(1)} %get-tuple-element.37), channel_id=1, replica_groups=mesh['expert'=32,'tensor'=8] {'expert'}, dimensions={0} | all-to-all | bytes 16777216 | tf_op jit(solution)/shard_map/all_to_all | solution.py:33
  244.1 7.7 %all-to-all-start.1 = ((bf16[32,32,4096]{2,1,0:T(8,128)(2,1)}), bf16[32,32,4096]{2,1,0:T(8,128)(2,1)}, u32[]{:S(2)}, u32[]{:S(2)}) async-start(bf16[32,32,4096]{2,1,0:T(8,128)(2,1)} %get-tuple-element.36), calls=%async_computation.1 | async-start | bytes 16777216 | tf_op jit(solution)/shard_map/all_to_all | solution.py:34
  251.9 0.9 dynamic-slice_reduce_fusion
  253.0 0.7 fusion.21
  253.7 4.3 compare_select_fusion.5
  258.1 0.7 fusion.20
  258.9 15.5 %select_select_fusion = s32[512]{0:T(512)S(1)} fusion(pred[512]{0:T(512)(128)(4,1)S(1)} %get-tuple-element.30, pred[512]{0:T(512)(128)(4,1)S(1)} %get-tuple-element.29, pred[512]{0:T(512)(128)(4,1)S(1)} %get-tuple-element.28, pred[512]{0:T(512)(128)(4,1)S(1)} %get-tuple-element.27, pred[512]{0:T(512)(128)(4,1)S(1)} %get-tuple-element.26, ...), kind=kLoop, calls=%fused_computation.88 | loop fusion | flops 12800 | bytes 16996 | tf_op jit(solution)/shard_map/gather | solution.py:40
  274.5 13.4 %gather_fusion.3 = bf16[512,4096]{1,0:T(8,128)(2,1)} fusion(bf16[1024,4096]{1,0:T(8,128)(2,1)} %bitcast.82, s32[1024]{0:T(1024)S(1)} %pad_clamp_fusion), kind=kCustom, calls=%fused_computation.3 | custom fusion | bytes 8390656 | tf_op jit(solution)/shard_map/gather | solution.py:41
  287.9 3.5 fusion.9
  291.5 1.3 fusion.22
  292.8 144.1 %all-to-all-done.1 = bf16[32,32,4096]{2,1,0:T(8,128)(2,1)} async-done(((bf16[32,32,4096]{2,1,0:T(8,128)(2,1)}), bf16[32,32,4096]{2,1,0:T(8,128)(2,1)}, u32[]{:S(2)}, u32[]{:S(2)}) %all-to-all-start.1) | async-done | bytes 8388640 | tf_op jit(solution)/shard_map/all_to_all | solution.py:34
  436.9 13.0 %gather_fusion.5 = bf16[512,4096]{1,0:T(8,128)(2,1)} fusion(bf16[1024,4096]{1,0:T(8,128)(2,1)} %bitcast.43, s32[1024]{0:T(1024)S(1)} %pad_clamp_fusion), kind=kCustom, calls=%fused_computation.5 | custom fusion | bytes 8390656 | tf_op jit(solution)/shard_map/gather | solution.py:42
  449.9 4.3 multiply_reduce_fusion
  454.2 5.1 bitcast_add_fusion
  459.4 3.9 fusion.23
  463.3 0.8 broadcast_multiply_fusion
  464.1 55.6 %reduce-scatter.2.cloned.1.call-done = f32[512,512]{0,1:T(8,128)} async-done(((f32[4096,512]{0,1:T(8,128)}), f32[512,512]{0,1:T(8,128)}) %reduce-scatter.2.cloned.1.call-update) | async-done | bytes 1048592 | tf_op jit(solution)/shard_map/reduce_scatter | solution.py:65
  519.7 4.6 scatter_custom_fusion
  524.3 10.2 %all-to-all-start.2 = ((f32[512,32,32]{0,2,1:T(8,128)}), f32[512,32,32]{0,2,1:T(8,128)S(1)}, u32[]{:S(2)}, u32[]{:S(2)}) async-start(f32[512,32,32]{0,2,1:T(8,128)} %bitcast.85), calls=%async_computation.3 | async-start | bytes 4194304 | tf_op jit(solution)/shard_map/all_to_all | solution.py:74
  534.6 5.0 convolution_convert_fusion.1
  539.6 2.6 convolution_convert_fusion
  542.2 56.2 %all-to-all-done.2 = f32[512,32,32]{0,2,1:T(8,128)S(1)} async-done(((f32[512,32,32]{0,2,1:T(8,128)}), f32[512,32,32]{0,2,1:T(8,128)S(1)}, u32[]{:S(2)}, u32[]{:S(2)}) %all-to-all-start.2) | async-done | bytes 2097184 | tf_op jit(solution)/shard_map/all_to_all | solution.py:74
  598.5 1.6 bitcast_select_fusion
  600.0 7.6 %scatter_custom_fusion.1 = f32[512,256]{0,1:T(8,128)S(1)} fusion(s32[1024]{0:T(1024)S(1)} %bitcast.91, f32[512,1024]{0,1:T(8,128)} %bitcast_select_fusion, f32[]{:T(128)} %constant.70.clone.1), kind=kCustom, calls=%fused_computation.14 | custom fusion | flops 524288 | bytes 2621444 | tf_op jit(solution)/shard_map/scatter-add | solution.py:78
  607.6 0.7 convert_bitcast_fusion
  608.4 115.8 %all-gather.2.cloned.1.call-done = f32[256,4096,16]{1,2,0:T(8,128)} async-done(((f32[1,4096,16]{1,2,0:T(8,128)}), f32[256,4096,16]{1,2,0:T(8,128)}) %all-gather.2.cloned.1.call-update) | async-done | bytes 67108880 | tf_op jit(solution)/shard_map/all_gather | solution.py:63
  724.1 21.8 %reduce_sum.49 = f32[4096,16]{0,1:T(8,128)} reduce(f32[256,4096,16]{1,2,0:T(8,128)} %all-gather.2.cloned.1.call-done, f32[]{:T(128)} %constant.70.clone.1), dimensions={0}, to_apply=%region_7.8 | reduce | flops 16711680 | bytes 67371008 | tf_op jit(solution)/shard_map/reduce_sum | solution.py:63
  (40 shorter events, 2.3 us)
Async XLA Ops:
  8.0 7.3 copy-start
  8.0 1.2 copy-start.2
  244.1 192.7 %all-to-all-start.1 = ((bf16[32,32,4096]{2,1,0:T(8,128)(2,1)}), bf16[32,32,4096]{2,1,0:T(8,128)(2,1)}, u32[]{:S(2)}, u32[]{:S(2)}) async-start(bf16[32,32,4096]{2,1,0:T(8,128)(2,1)} %get-tuple-element.36), calls=%async_computation.1 | async-start | bytes 16777216 | tf_op jit(solution)/shard_map/all_to_all | solution.py:34
  251.8 267.9 %reduce-scatter.2.cloned.1.call-start = ((), (), s32[]{:S(2)}) async-start(), calls=%async_computation.4 | async-start | bytes 9437184 | tf_op jit(solution)/shard_map/reduce_scatter | solution.py:65
  274.5 16.9 %copy-start.5 = (bf16[4096,256]{1,0:T(8,128)(2,1)S(1)}, bf16[4096,256]{1,0:T(8,128)(2,1)}, u32[]{:S(2)}) copy-start(bf16[4096,256]{1,0:T(8,128)(2,1)} %param.8) | copy-start | bytes 6291460
  287.9 3.5 copy-start.3
  459.3 264.9 %all-gather.2.cloned.1.call-start = ((), (), s32[]{:S(2)}) async-start(), calls=%async_computation.5 | async-start | bytes 67371008 | tf_op jit(solution)/shard_map/all_gather | solution.py:63
  524.3 74.1 %all-to-all-start.2 = ((f32[512,32,32]{0,2,1:T(8,128)}), f32[512,32,32]{0,2,1:T(8,128)S(1)}, u32[]{:S(2)}, u32[]{:S(2)}) async-start(f32[512,32,32]{0,2,1:T(8,128)} %bitcast.85), calls=%async_computation.3 | async-start | bytes 4194304 | tf_op jit(solution)/shard_map/all_to_all | solution.py:74
  534.6 5.0 copy-start.4
  724.1 21.8 %copy-start.1 = (bf16[256,4096]{1,0:T(8,128)(2,1)S(1)}, bf16[256,4096]{1,0:T(8,128)(2,1)}, u32[]{:S(2)}) copy-start(bf16[256,4096]{1,0:T(8,128)(2,1)} %param.7) | copy-start | bytes 6291460
Sparse Core Ops, SparseCore 0:
  459.4 60.2 reduce-scatter.1
Sparse Core Ops, SparseCore 1:
  464.2 259.9 all-gather.1
